TPU v7x, 32 devices: a whole 2x2x4 slice. The times are simulated.
32 devices in a mesh: task: 4 (over x, core), tensor: 4 (over z), dp: 2 (over y).
Axes of the slice: x: 2, y: 2, z: 4, core: 2. Of those that a mesh axis runs over, the one named last changes fastest.
Arguments:
- hidden: bfloat16 [1024, 4608], P(('task', 'dp')), may hold values from -6 to 6
- pre_gain: float32 [4608], replicated, may hold values from 0.1 to 1.9
- base_query: bfloat16 [4608, 512], P('dp', 'tensor'), may hold values from -0.09375 to 0.09375
- base_keyval: bfloat16 [2, 4608, 256], P(None, 'dp', 'tensor'), may hold values from -0.09375 to 0.09375
- base_output: bfloat16 [512, 4608], P('tensor', 'dp'), may hold values from -0.25 to 0.25
- delta_query: bfloat16 [4, 4608, 512], P('task', 'dp', 'tensor'), may hold values from -0.046875 to 0.046875
- delta_keyval: bfloat16 [4, 2, 4608, 256], P('task', None, 'dp', 'tensor'), may hold values from -0.046875 to 0.046875
- delta_output: bfloat16 [4, 512, 4608], P('task', 'tensor', 'dp'), may hold values from -0.125 to 0.125
- trim_query: int32 [4, 72, 8], P('task', 'dp', 'tensor'), may hold values 0 or 1
- trim_keyval: int32 [4, 2, 72, 4], P('task', None, 'dp', 'tensor'), may hold values 0 or 1
- trim_output: int32 [4, 8, 72], P('task', 'tensor', 'dp'), may hold values 0 or 1
- sign_query: int32 [72, 8], P('dp', 'tensor'), may hold values from 0 to 1
- sign_keyval: int32 [2, 72, 4], P(None, 'dp', 'tensor'), may hold values from 0 to 1
- sign_output: int32 [8, 72], P('tensor', 'dp'), may hold values from 0 to 1
- post_gain: float32 [4608], replicated, may hold values from 0.1 to 1.9
- final_gain: float32 [4608], replicated, may hold values from 0.1 to 1.9
- unembedding: bfloat16 [28672, 4608], P(('task', 'tensor', 'dp')), may hold values from -0.375 to 0.375
- targets: int32 [1024], replicated, may hold values from 0 to 28671
- loss_mask: int32 [1024], replicated, may hold values 0 or 1
Outputs:
- token_loss: float32 [1024], P(('task', 'dp'))
- summary: float32 [2], replicated
All inputs are finite; a program needn't handle non-finite values. No bound on the sum of `trim_query` or of `trim_keyval` or of `trim_output` on one device may be relied on, other than what follows from the above.
Results may differ from a plain program's by a relative error of at most 0.0045.
Values may be sent and summed in bfloat16 or wider, within the bound.
No kernel may reach another device: no remote copies, remote signals or barrier semaphores. Data moves between devices by JAX's collectives and lax.ppermute only.
A program may use at most 128 MiB of HBM per device.

v0:
```python
import jax
import jax.numpy as jnp
from jax import lax
from jax.sharding import PartitionSpec as P

BLK = 64
EPSILON = 1e-06
QUERY_SCALE = 1.0 / 12.0
ROPE_BASE = 10000.0
SCORE_CAP = 50.0
LOGIT_CAP = 30.0


def from_partner(block, axis, bit):
    count = lax.axis_size(axis)
    route = []
    for low in range(count):
        high = low | 1 << bit
        if high != low and high < count:
            route += [(low, high), (high, low)]
    return lax.ppermute(block, axis, route)


def trim_delta(deltas, trim_bits, sign_bits):
    layout = deltas.shape
    row_blocks = layout[-2] // BLK
    col_blocks = layout[-1] // BLK
    blocks = deltas.reshape(layout[:-2] + (row_blocks, BLK, col_blocks, BLK))
    wanted = (2 * sign_bits - 1).astype(jnp.float32)[..., :, None, :, None]
    keeping = (trim_bits[..., :, None, :, None] == 1) & (
        jnp.sign(blocks.astype(jnp.float32)) == wanted
    )
    return jnp.where(keeping, blocks, jnp.zeros_like(blocks)).reshape(layout)


def finish_merge(base_part, totals, counts):
    return (base_part.astype(jnp.float32) + totals / jnp.maximum(counts, 1.0)).astype(jnp.bfloat16)


def merge_every(base_part, gathered):
    totals = jnp.sum(gathered.astype(jnp.float32), axis=0)
    counts = jnp.sum((gathered != 0).astype(jnp.float32), axis=0)
    return finish_merge(base_part, totals, counts)


def rms_norm(values, gain):
    scale = lax.rsqrt(jnp.mean(values * values, axis=-1, keepdims=True) + EPSILON)
    return values * scale * gain


def rotate(values, angles):
    half_width = values.shape[-1] // 2
    first = values[..., :half_width]
    second = values[..., half_width:]
    cosine = jnp.cos(angles)
    sine = jnp.sin(angles)
    return jnp.concatenate(
        [first * cosine - second * sine, second * cosine + first * sine], axis=-1
    )


def on_device(
    hidden,
    pre_gain,
    base_query,
    base_keyval,
    base_output,
    delta_query,
    delta_keyval,
    delta_output,
    trim_query,
    trim_keyval,
    trim_output,
    sign_query,
    sign_keyval,
    sign_output,
    post_gain,
    final_gain,
    unembedding,
    targets,
    loss_mask,
):
    kept_query = trim_delta(delta_query, trim_query, sign_query)
    kept_keyval = trim_delta(delta_keyval, trim_keyval, sign_keyval)
    kept_output = trim_delta(delta_output, trim_output, sign_output)
    gathered = (
        lax.all_gather(kept_query, "task", axis=0, tiled=True),
        lax.all_gather(kept_keyval, "task", axis=0, tiled=True),
        lax.all_gather(kept_output, "task", axis=0, tiled=True),
    )
    halves = (
        merge_every(base_query, gathered[0]),
        merge_every(base_keyval, gathered[1]),
        merge_every(base_output, gathered[2]),
    )
    merged_query, merged_keyval, merged_output = (
        lax.all_gather(halves[0], "dp", axis=0, tiled=True),
        lax.all_gather(halves[1], "dp", axis=1, tiled=True),
        lax.all_gather(halves[2], "dp", axis=1, tiled=True),
    )
    residual = hidden.astype(jnp.float32)
    normed = rms_norm(residual, pre_gain).astype(jnp.bfloat16)
    row_count = residual.shape[0]
    group_index = lax.axis_index(("task", "dp"))
    query_positions = group_index * row_count + jnp.arange(row_count, dtype=jnp.int32)
    head_width = merged_query.shape[1]
    frequencies = jnp.exp(
        -jnp.log(ROPE_BASE)
        * 2.0
        * jnp.arange(head_width // 2, dtype=jnp.int32).astype(jnp.float32)
        / head_width
    )
    angles = query_positions.astype(jnp.float32)[:, None] * frequencies[None, :]
    queries = jnp.dot(normed, merged_query, preferred_element_type=jnp.float32)
    queries = (rotate(queries, angles) * QUERY_SCALE).astype(jnp.bfloat16)
    key_half = jnp.dot(normed, merged_keyval[0], preferred_element_type=jnp.float32)
    value_half = jnp.dot(normed, merged_keyval[1], preferred_element_type=jnp.float32)
    other_key, other_value = (
        from_partner(key_half.astype(jnp.bfloat16), "tensor", 0).astype(key_half.dtype),
        from_partner(value_half.astype(jnp.bfloat16), "tensor", 0).astype(value_half.dtype),
    )
    is_lower = lax.axis_index("tensor") % 2 == 0
    keys_full = jnp.where(
        is_lower,
        jnp.concatenate([key_half, other_key], axis=1),
        jnp.concatenate([other_key, key_half], axis=1),
    )
    values_full = jnp.where(
        is_lower,
        jnp.concatenate([value_half, other_value], axis=1),
        jnp.concatenate([other_value, value_half], axis=1),
    )
    keys_full = rotate(keys_full, angles).astype(jnp.bfloat16)
    values_full = values_full.astype(jnp.bfloat16)
    key_piece = lax.all_gather(keys_full, ("task", "dp"), axis=0, tiled=True)
    value_piece = lax.all_gather(values_full, ("task", "dp"), axis=0, tiled=True)
    scores = lax.dot_general(
        queries, key_piece, (((1,), (1,)), ((), ())), preferred_element_type=jnp.float32
    )
    capped = SCORE_CAP * jnp.tanh(scores / SCORE_CAP)
    key_positions = jnp.arange(key_piece.shape[0], dtype=jnp.int32)
    allowed = key_positions[None, :] <= query_positions[:, None]
    weights = jnp.where(allowed, jnp.exp(capped), 0.0)
    numerator = jnp.dot(
        weights.astype(jnp.bfloat16), value_piece, preferred_element_type=jnp.float32
    )
    denominator = jnp.sum(weights, axis=1)
    numerator, denominator = (numerator, denominator)
    attention = (numerator / denominator[:, None]).astype(jnp.bfloat16)
    partial_value = jnp.dot(attention, merged_output, preferred_element_type=jnp.float32)
    task_count = lax.axis_size("task")
    tensor_count = lax.axis_size("tensor")
    dp_count = lax.axis_size("dp")
    span_rows = row_count // tensor_count
    share_rows = lax.psum_scatter(
        partial_value.astype(jnp.bfloat16), "tensor", scatter_dimension=0, tiled=True
    ).astype(jnp.float32)
    own_stream = lax.dynamic_slice_in_dim(
        residual, lax.axis_index("tensor") * span_rows, span_rows, 0
    )
    stream = own_stream + rms_norm(share_rows, post_gain)
    final = rms_norm(stream, final_gain).astype(jnp.bfloat16)
    every_rows = lax.all_gather(final, ("task", "tensor", "dp"), axis=0, tiled=True)
    ordered_targets = jnp.transpose(
        targets.reshape(task_count, dp_count, tensor_count, span_rows), (0, 2, 1, 3)
    ).reshape(-1)
    ordered_mask = jnp.transpose(
        loss_mask.reshape(task_count, dp_count, tensor_count, span_rows), (0, 2, 1, 3)
    ).reshape(-1)
    logits = lax.dot_general(
        every_rows, unembedding, (((1,), (1,)), ((), ())), preferred_element_type=jnp.float32
    )
    capped = LOGIT_CAP * jnp.tanh(logits / LOGIT_CAP)
    vocab_ids = lax.axis_index(("task", "tensor", "dp")) * unembedding.shape[0] + jnp.arange(
        unembedding.shape[0], dtype=jnp.int32
    )
    local_sumexp = jnp.sum(jnp.exp(capped), axis=1)
    local_target = jnp.sum(
        jnp.where(ordered_targets[:, None] == vocab_ids[None, :], capped, 0.0), axis=1
    )
    sumexp, target_logit = lax.psum((local_sumexp, local_target), ("task", "tensor", "dp"))
    counted = ordered_mask.astype(jnp.float32)
    losses = (jnp.log(sumexp) - target_logit) * counted
    summary = jnp.stack([jnp.sum(losses), jnp.sum(counted)])
    losses = jnp.transpose(
        losses.reshape(task_count, tensor_count, dp_count, span_rows), (0, 2, 1, 3)
    ).reshape(-1)
    own_losses = lax.dynamic_slice_in_dim(losses, group_index * row_count, row_count, 0)
    return (own_losses, summary)


def solution(mesh):
    return jax.shard_map(
        on_device,
        mesh=mesh,
        in_specs=(
            P(("task", "dp"), None),
            P(),
            P("dp", "tensor"),
            P(None, "dp", "tensor"),
            P("tensor", "dp"),
            P("task", "dp", "tensor"),
            P("task", None, "dp", "tensor"),
            P("task", "tensor", "dp"),
            P("task", "dp", "tensor"),
            P("task", None, "dp", "tensor"),
            P("task", "tensor", "dp"),
            P("dp", "tensor"),
            P(None, "dp", "tensor"),
            P("tensor", "dp"),
            P(),
            P(),
            P(("task", "tensor", "dp"), None),
            P(),
            P(),
        ),
        out_specs=(P(("task", "dp")), P()),
        check_vma=False,
    )
```

profile of v0, /device:TPU:0, one launch (start us, length us, event | category | flops | bytes accessed | tf_op | source)
XLA Modules:
  0.0 354.9 jit_solution(13832820005379422890)
XLA Ops:
  7.2 0.7 add_convert_fusion.4
  8.0 0.1 eq.117
  8.1 0.7 broadcast_compare_fusion
  8.8 0.1 and.54
  8.9 2.6 fusion.7
  11.7 0.1 copy.38
  11.8 0.7 eq.108
  12.5 1.3 eq.109
  13.8 0.4 copy.39
  14.1 0.3 copy-done.15
  14.4 0.2 and.49
  14.7 0.8 and.50
  15.5 0.2 copy.37
  15.7 0.6 fusion.5
  16.3 1.1 copy.41
  17.5 0.1 copy.44
  17.6 0.7 eq.123
  18.3 1.3 eq.124
  19.6 0.4 copy.45
  20.0 0.3 copy-done.16
  20.3 0.2 and.57
  20.5 0.8 and.58
  21.3 0.1 copy-done.6
  21.4 1.4 fusion.9
  22.8 1.1 copy.36
  24.0 0.3 multiply_reduce_fusion
  24.3 14.2 %all-gather.12.cloned.1.call-done = bf16[4,2,2304,64]{2,3,1,0:T(8,128)(2,1)} async-done(((bf16[1,2,2304,64]{2,3,1,0:T(8,128)(2,1)}), bf16[4,2,2304,64]{2,3,1,0:T(8,128)(2,1)}) %all-gather.12.cloned.1.call-update) | async-done | bytes 2359312 | tf_op jit(solution)/shard_map/all_gather | solution.py:88
  38.5 3.6 %convert_reduce_fusion.2 = (f32[2,2304,64]{1,2,0:T(8,128)S(1)}, f32[2,2304,64]{1,2,0:T(8,128)S(1)}) fusion(bf16[4,2,2304,64]{2,3,1,0:T(8,128)(2,1)} %all-gather.12.cloned.1.call-done), kind=kLoop, calls=%fused_computation.3 | loop fusion | flops 5308416 | bytes 4718592 | tf_op jit(solution)/shard_map/reduce_sum | solution.py:42
  42.2 1.1 add_convert_fusion.1
  43.3 0.2 all-gather.10.cloned.1.call-start
  43.5 20.6 %all-gather.8.cloned.1.call-done = bf16[4,2304,128]{2,1,0:T(8,128)(2,1)} async-done(((bf16[1,2304,128]{2,1,0:T(8,128)(2,1)}), bf16[4,2304,128]{2,1,0:T(8,128)(2,1)}) %all-gather.8.cloned.1.call-update) | async-done | bytes 2359312 | tf_op jit(solution)/shard_map/all_gather | solution.py:87
  64.2 4.6 %convert_reduce_fusion.4 = (f32[2304,128]{1,0:T(8,128)}, f32[2304,128]{1,0:T(8,128)S(1)}) fusion(bf16[4,2304,128]{2,1,0:T(8,128)(2,1)} %all-gather.8.cloned.1.call-done), kind=kLoop, calls=%fused_computation.5 | loop fusion | flops 5308416 | bytes 4718592 | tf_op jit(solution)/shard_map/reduce_sum | solution.py:42
  68.8 0.4 copy.50
  69.1 1.6 copy.51
  70.8 2.2 add_convert_fusion.2
  73.1 16.7 %all-gather.16.cloned.1.call-done = bf16[4,128,2304]{2,1,0:T(8,128)(2,1)} async-done(((bf16[1,128,2304]{2,1,0:T(8,128)(2,1)}), bf16[4,128,2304]{2,1,0:T(8,128)(2,1)}) %all-gather.16.cloned.1.call-update) | async-done | bytes 2359312 | tf_op jit(solution)/shard_map/all_gather | solution.py:89
  89.8 3.6 %convert_reduce_fusion = (f32[128,2304]{1,0:T(8,128)S(1)}, f32[128,2304]{1,0:T(8,128)S(1)}) fusion(bf16[4,128,2304]{2,1,0:T(8,128)(2,1)} %all-gather.16.cloned.1.call-done), kind=kLoop, calls=%fused_computation.1 | loop fusion | flops 5308416 | bytes 4718592 | tf_op jit(solution)/shard_map/reduce_sum | solution.py:42
  93.5 1.1 add_convert_fusion
  94.6 19.4 %all-gather.14.cloned.1.call-done = bf16[2,4608,64]{1,2,0:T(8,128)(2,1)} async-done(((bf16[2,2304,64]{1,2,0:T(8,128)(2,1)}), bf16[2,4608,64]{1,2,0:T(8,128)(2,1)}) %all-gather.14.cloned.1.call-update) | async-done | bytes 1179664 | tf_op jit(solution)/shard_map/all_gather | solution.py:98
  114.0 1.8 fusion.42
  115.8 1.6 collective-permute-start
  117.3 0.6 fusion.14
  117.9 0.6 collective-permute-start.1
  118.5 19.6 %all-gather.10.cloned.1.call-done = bf16[4608,128]{0,1:T(8,128)(2,1)} async-done(((bf16[2304,128]{0,1:T(8,128)(2,1)}), bf16[4608,128]{0,1:T(8,128)(2,1)}) %all-gather.10.cloned.1.call-update) | async-done | bytes 1179664 | tf_op jit(solution)/shard_map/all_gather | solution.py:97
  138.2 1.8 fusion.40
  140.0 0.2 fusion.28
  140.3 16.4 %all_gather.31 = bf16[1024,128]{0,1:T(8,128)(2,1)S(1)} all-gather(bf16[128,128]{0,1:T(8,128)(2,1)S(1)} %pad_maximum_fusion), channel_id=1, replica_groups=mesh['task'=4,'tensor'=4,'dp'=2] {'task','dp'}, dimensions={0}, use_global_device_ids=true | all-gather | bytes 294912 | tf_op jit(solution)/shard_map/all_gather | solution.py:135
  156.7 17.9 %all_gather.32 = bf16[1024,128]{0,1:T(8,128)(2,1)S(1)} all-gather(bf16[128,128]{0,1:T(8,128)(2,1)S(1)} %fusion.19), channel_id=1, replica_groups=mesh['task'=4,'tensor'=4,'dp'=2] {'task','dp'}, dimensions={0}, use_global_device_ids=true | all-gather | bytes 294912 | tf_op jit(solution)/shard_map/all_gather | solution.py:136
  174.6 0.4 fusion.43
  175.1 3.1 convolution_convert_fusion
  178.2 0.2 convert_element_type.132
  178.5 29.2 %reduce-scatter.2.cloned.1.call-done = bf16[32,4608]{1,0:T(8,128)(2,1)} async-done(((bf16[128,4608]{1,0:T(8,128)(2,1)}), bf16[32,4608]{1,0:T(8,128)(2,1)}) %reduce-scatter.2.cloned.1.call-update) | async-done | bytes 294928 | tf_op jit(solution)/shard_map/reduce_scatter | solution.py:155
  207.7 1.2 fusion.11
  208.9 1.3 multiply_reduce_fusion.1
  210.2 0.9 multiply_convert_fusion.1
  211.2 0.1 eq.126
  211.4 0.1 convert_element_type.168
  211.5 0.6 convert_reduce_fusion.6
  212.1 79.2 %all-gather.20.cloned.1.call-done = bf16[1024,4608]{1,0:T(8,128)(2,1)} async-done(((bf16[32,4608]{1,0:T(8,128)(2,1)}), bf16[1024,4608]{1,0:T(8,128)(2,1)}) %all-gather.20.cloned.1.call-update) | async-done | bytes 9437200 | tf_op jit(solution)/shard_map/all_gather | solution.py:163
  291.4 14.4 %exponential_reduce_fusion = (f32[1024]{0:T(1024)S(1)}, f32[1024]{0:T(1024)S(1)}) fusion(s32[896]{0:T(1024)S(1)} %iota_add_fusion, s32[1024]{0:T(1024)S(1)} %eq.126, bf16[1024,4608]{1,0:T(8,128)(2,1)} %all-gather.20.cloned.1.call-done, bf16[896,4608]{1,0:T(8,128)(2,1)} %param.35), kind=kOutput, calls=%fused_computation.8 | convolution fusion | flops 8461219840 | bytes 17710592 | tf_op jit(solution)/shard_map/dot_general | solution.py:170
  305.7 39.1 %all-reduce = (f32[1024]{0:T(1024)S(1)}, f32[1024]{0:T(1024)S(1)}) all-reduce(f32[1024]{0:T(1024)S(1)} %get-tuple-element.3, f32[1024]{0:T(1024)S(1)} %get-tuple-element.2), channel_id=1, replica_groups=mesh['task'=4,'tensor'=4,'dp'=2] {'task','tensor','dp'}, use_global_device_ids=true, to_apply=%region_14.15 | all-reduce | flops 2048 | bytes 16384 | tf_op jit(solution)/shard_map/psum | solution.py:181
  344.8 0.6 fusion.41
  345.6 0.6 dynamic_slice.7
  346.2 1.8 pad_maximum_fusion.1
  (75 shorter events, 1.2 us)
Async XLA Ops:
  7.2 4.5 %copy-start.11 = (s32[36,2]{0,1:T(2,128)S(1)}, s32[36,2]{0,1:T(2,128)}, u32[]{:S(2)}) copy-start(s32[36,2]{0,1:T(2,128)} %param.30) | copy-start | bytes 868
  7.2 31.4 %all-gather.12.cloned.1.call-start = ((), (), s32[]{:S(2)}) async-start(), calls=%async_computation.3 | async-start | bytes 2949120 | tf_op jit(solution)/shard_map/all_gather | solution.py:88
  11.6 52.6 %all-gather.8.cloned.1.call-start = ((), (), s32[]{:S(2)}) async-start(), calls=%async_computation.1 | async-start | bytes 2949120 | tf_op jit(solution)/shard_map/all_gather | solution.py:87
  13.7 0.7 copy-start.15
  14.4 1.1 copy-start.4
  16.3 1.2 copy-start.12
  17.4 72.4 %all-gather.16.cloned.1.call-start = ((), (), s32[]{:S(2)}) async-start(), calls=%async_computation.5 | async-start | bytes 2949120 | tf_op jit(solution)/shard_map/all_gather | solution.py:89
  19.6 0.7 copy-start.16
  20.3 1.1 copy-start.6
  21.4 1.5 copy-start.5
  22.7 1.3 copy-start
  22.7 91.3 %all-gather.14.cloned.1.call-start = ((), (), s32[]{:S(2)}) async-start(), calls=%async_computation.4 | async-start | bytes 1769472 | tf_op jit(solution)/shard_map/all_gather | solution.py:98
  24.3 17.9 %copy-start.2 = (bf16[2,2304,64]{1,2,0:T(8,128)(2,1)S(1)}, bf16[2,2304,64]{1,2,0:T(8,128)(2,1)}, u32[]{:S(2)}) copy-start(bf16[2,2304,64]{1,2,0:T(8,128)(2,1)} %param.22) | copy-start | bytes 1769476
  43.3 94.9 %all-gather.10.cloned.1.call-start = ((), (), s32[]{:S(2)}) async-start(), calls=%async_computation.2 | async-start | bytes 1769472 | tf_op jit(solution)/shard_map/all_gather | solution.py:97
  73.0 102.1 %all-gather.18.cloned.1.call-start = ((), (), s32[]{:S(2)}) async-start(), calls=%async_computation.6 | async-start | bytes 1769472 | tf_op jit(solution)/shard_map/all_gather | solution.py:99
  73.1 20.4 %copy-start.3 = (bf16[128,2304]{1,0:T(8,128)(2,1)S(1)}, bf16[128,2304]{1,0:T(8,128)(2,1)}, u32[]{:S(2)}) copy-start(bf16[128,2304]{1,0:T(8,128)(2,1)} %param.23) | copy-start | bytes 1769476
  93.5 20.5 %copy-start.14 = (f32[4608]{0:T(1024)S(1)}, f32[4608]{0:T(1024)}, u32[]{:S(2)}) copy-start(f32[4608]{0:T(1024)} %param.20) | copy-start | bytes 55300
  94.6 113.1 %reduce-scatter.2.cloned.1.call-start = ((), (), s32[]{:S(2)}) async-start(), calls=%async_computation.7 | async-start | bytes 1474560 | tf_op jit(solution)/shard_map/reduce_scatter | solution.py:155
  114.0 3.3 copy-start.13
  115.8 24.2 %collective-permute-start = (bf16[128,64]{0,1:T(8,128)(2,1)S(1)}, bf16[128,64]{0,1:T(8,128)(2,1)S(1)}, u32[]{:S(2)}, u32[]{:S(2)}) collective-permute-start(bf16[128,64]{0,1:T(8,128)(2,1)S(1)} %get-tuple-element.20), channel_id=1, source_target_pairs={{0,2},{2,0},{4,6},{6,4},{1,3},{3,1},{5,7},{7,5},{8,10},{10,8},{12,... | collective-permute-start | bytes 49160 | tf_op jit(solution)/shard_map/ppermute | solution.py:21
  117.9 38.8 %collective-permute-start.1 = (bf16[128,64]{0,1:T(8,128)(2,1)S(1)}, bf16[128,64]{0,1:T(8,128)(2,1)S(1)}, u32[]{:S(2)}, u32[]{:S(2)}) collective-permute-start(bf16[128,64]{0,1:T(8,128)(2,1)S(1)} %fusion.14), channel_id=1, source_target_pairs={{0,2},{2,0},{4,6},{6,4},{1,3},{3,1},{5,7},{7,5},{8,10},{10,8},{12,... | collective-permute-start | bytes 49160 | tf_op jit(solution)/shard_map/ppermute | solution.py:21
  178.2 113.2 %all-gather.20.cloned.1.call-start = ((), (), s32[]{:S(2)}) async-start(), calls=%async_computation.8 | async-start | bytes 9732096 | tf_op jit(solution)/shard_map/all_gather | solution.py:163
  178.5 31.7 %copy-start.7 = (f32[4608]{0:T(1024)S(1)}, f32[4608]{0:T(1024)}, u32[]{:S(2)}) copy-start(f32[4608]{0:T(1024)} %param.33) | copy-start | bytes 55300
  178.5 31.7 %copy-start.8 = (f32[4608]{0:T(1024)S(1)}, f32[4608]{0:T(1024)}, u32[]{:S(2)}) copy-start(f32[4608]{0:T(1024)} %param.34) | copy-start | bytes 55300
  207.7 2.5 copy-start.1
  208.9 2.3 copy-start.10
  208.9 2.5 copy-start.9
Sparse Core Ops, SparseCore 0:
  11.7 26.7 all-gather.11
  40.1 24.0 all-gather.7
  65.7 24.0 all-gather.15
  91.2 22.7 all-gather.13
  115.4 22.7 all-gather.9
  139.6 24.4 all-gather.17
  178.3 29.3 reduce-scatter.1
  211.3 80.0 all-gather.19
where the time goes:
time: 356 us; the launch traced here: 355 us
  waiting for transfers between devices  199 us (56%)
  blocking collectives  73.5 us (21%)
  other arithmetic  29.4 us (8%)
  matrix products  22 us (6%)
  between operations  14.6 us (4%)
  local copies, waits for them, and re-layouts  13.6 us (4%)
    all_gather x1, waiting for transfers between devices, on_device(): lax.all_gather(final, ('task', 'tensor', 'dp'), axis=0, tiled=True)  79.2 us
    psum x1, blocking collectives, on_device(): lax.psum((local_sumexp, local_target), ('task', 'tensor', 'dp'))  39.1 us
    reduce_scatter x1, waiting for transfers between devices, on_device(): lax.psum_scatter(partial_value.astype(jnp.bfloat16), 'tensor', scatter_di...  29.2 us
    all_gather x1, waiting for transfers between devices, on_device(): lax.all_gather(kept_query, 'task', axis=0, tiled=True)  20.6 us
    all_gather x1, waiting for transfers between devices, on_device(): lax.all_gather(halves[0], 'dp', axis=0, tiled=True)  19.6 us
    all_gather x1, waiting for transfers between devices, on_device(): lax.all_gather(halves[1], 'dp', axis=1, tiled=True)  19.4 us
    all_gather x1, blocking collectives, on_device(): lax.all_gather(values_full, ('task', 'dp'), axis=0, tiled=True)  17.9 us
    all_gather x1, waiting for transfers between devices, on_device(): lax.all_gather(kept_output, 'task', axis=0, tiled=True)  16.7 us
  transfers between devices with their start and end apart: 10, of which 7 were waited for; matrix products, arithmetic and copies ran while one was open for 10% of the time, Pallas kernels for 0%

commit v1 on v0

--- a/solution.py
+++ b/solution.py
@@ -9,6 +9,14 @@
 ROPE_BASE = 10000.0
 SCORE_CAP = 50.0
 LOGIT_CAP = 30.0
+
+
+def tasks_try_all(a0):
+    axis_id = ("tensor", "dp")
+    group_axis = "task"
+    for hop_no in (axis_id, group_axis):
+        a0 = lax.psum(a0, hop_no)
+    return a0
 
 
 def from_partner(block, axis, bit):
@@ -178,7 +186,7 @@
     local_target = jnp.sum(
         jnp.where(ordered_targets[:, None] == vocab_ids[None, :], capped, 0.0), axis=1
     )
-    sumexp, target_logit = lax.psum((local_sumexp, local_target), ("task", "tensor", "dp"))
+    sumexp, target_logit = tasks_try_all((local_sumexp, local_target))
     counted = ordered_mask.astype(jnp.float32)
     losses = (jnp.log(sumexp) - target_logit) * counted
     summary = jnp.stack([jnp.sum(losses), jnp.sum(counted)])

time: 356 us -> 343 us (0.963)
  blocking collectives: 73.5 us -> 60.6 us
    psum x1 -> x2, blocking collectives: 39.1 us -> 26.3 us  [tasks_try_all(): a0 = lax.psum(a0, hop_no)]
  transfers between devices with their start and end apart: 10 -> 10, of which waited for: 7 -> 7; matrix products, arithmetic and copies ran while one was open for 10% -> 11% of each run, Pallas kernels for 0% -> 0%
where the time goes in v1:
time: 343 us; the launch traced here: 342 us
  waiting for transfers between devices  199 us (58%)
  blocking collectives  60.6 us (18%)
  other arithmetic  29.5 us (9%)
  matrix products  22 us (6%)
  between operations  14.6 us (4%)
  local copies, waits for them, and re-layouts  13.6 us (4%)
    all_gather x1, waiting for transfers between devices, on_device(): lax.all_gather(final, ('task', 'tensor', 'dp'), axis=0, tiled=True)  79.2 us
    reduce_scatter x1, waiting for transfers between devices, on_device(): lax.psum_scatter(partial_value.astype(jnp.bfloat16), 'tensor', scatter_di...  29.1 us
    psum x2, blocking collectives, tasks_try_all(): a0 = lax.psum(a0, hop_no)  26.3 us
    all_gather x1, waiting for transfers between devices, on_device(): lax.all_gather(kept_query, 'task', axis=0, tiled=True)  20.7 us
    all_gather x1, waiting for transfers between devices, on_device(): lax.all_gather(halves[0], 'dp', axis=0, tiled=True)  19.6 us
    all_gather x1, waiting for transfers between devices, on_device(): lax.all_gather(halves[1], 'dp', axis=1, tiled=True)  19.3 us
    all_gather x1, blocking collectives, on_device(): lax.all_gather(values_full, ('task', 'dp'), axis=0, tiled=True)  17.9 us
    all_gather x1, waiting for transfers between devices, on_device(): lax.all_gather(kept_output, 'task', axis=0, tiled=True)  16.7 us
  transfers between devices with their start and end apart: 10, of which 7 were waited for; matrix products, arithmetic and copies ran while one was open for 11% of the time, Pallas kernels for 0%

profile of v1, /device:TPU:0, one launch (start us, length us, event | category | flops | bytes accessed | tf_op | source)
XLA Modules:
  0.0 342.0 jit_solution(7970432330395294881)
XLA Ops:
  7.2 0.7 add_convert_fusion.4
  8.0 0.1 eq.117
  8.1 0.7 broadcast_compare_fusion
  8.8 0.1 and.54
  8.9 2.6 fusion.7
  11.7 0.1 copy.38
  11.8 0.7 eq.108
  12.4 1.3 eq.109
  13.7 0.4 copy.39
  14.1 0.3 copy-done.15
  14.4 0.2 and.49
  14.7 0.8 and.50
  15.5 0.2 copy.37
  15.7 0.6 fusion.5
  16.3 1.1 copy.41
  17.5 0.1 copy.44
  17.6 0.7 eq.123
  18.3 1.3 eq.124
  19.6 0.4 copy.45
  20.0 0.3 copy-done.16
  20.3 0.2 and.57
  20.5 0.8 and.58
  21.4 1.4 fusion.9
  22.8 1.2 copy.36
  24.0 0.3 multiply_reduce_fusion
  24.3 14.2 %all-gather.12.cloned.1.call-done = bf16[4,2,2304,64]{2,3,1,0:T(8,128)(2,1)} async-done(((bf16[1,2,2304,64]{2,3,1,0:T(8,128)(2,1)}), bf16[4,2,2304,64]{2,3,1,0:T(8,128)(2,1)}) %all-gather.12.cloned.1.call-update) | async-done | bytes 2359312 | tf_op jit(solution)/shard_map/all_gather | solution.py:96
  38.5 3.6 %convert_reduce_fusion.2 = (f32[2,2304,64]{1,2,0:T(8,128)S(1)}, f32[2,2304,64]{1,2,0:T(8,128)S(1)}) fusion(bf16[4,2,2304,64]{2,3,1,0:T(8,128)(2,1)} %all-gather.12.cloned.1.call-done), kind=kLoop, calls=%fused_computation.3 | loop fusion | flops 5308416 | bytes 4718592 | tf_op jit(solution)/shard_map/reduce_sum | solution.py:50
  42.2 1.1 add_convert_fusion.1
  43.3 0.2 all-gather.10.cloned.1.call-start
  43.5 20.7 %all-gather.8.cloned.1.call-done = bf16[4,2304,128]{2,1,0:T(8,128)(2,1)} async-done(((bf16[1,2304,128]{2,1,0:T(8,128)(2,1)}), bf16[4,2304,128]{2,1,0:T(8,128)(2,1)}) %all-gather.8.cloned.1.call-update) | async-done | bytes 2359312 | tf_op jit(solution)/shard_map/all_gather | solution.py:95
  64.2 4.6 %convert_reduce_fusion.4 = (f32[2304,128]{1,0:T(8,128)}, f32[2304,128]{1,0:T(8,128)S(1)}) fusion(bf16[4,2304,128]{2,1,0:T(8,128)(2,1)} %all-gather.8.cloned.1.call-done), kind=kLoop, calls=%fused_computation.5 | loop fusion | flops 5308416 | bytes 4718592 | tf_op jit(solution)/shard_map/reduce_sum | solution.py:50
  68.8 0.4 copy.50
  69.1 1.6 copy.51
  70.8 2.2 add_convert_fusion.2
  73.1 16.7 %all-gather.16.cloned.1.call-done = bf16[4,128,2304]{2,1,0:T(8,128)(2,1)} async-done(((bf16[1,128,2304]{2,1,0:T(8,128)(2,1)}), bf16[4,128,2304]{2,1,0:T(8,128)(2,1)}) %all-gather.16.cloned.1.call-update) | async-done | bytes 2359312 | tf_op jit(solution)/shard_map/all_gather | solution.py:97
  89.8 3.6 %convert_reduce_fusion = (f32[128,2304]{1,0:T(8,128)S(1)}, f32[128,2304]{1,0:T(8,128)S(1)}) fusion(bf16[4,128,2304]{2,1,0:T(8,128)(2,1)} %all-gather.16.cloned.1.call-done), kind=kLoop, calls=%fused_computation.1 | loop fusion | flops 5308416 | bytes 4718592 | tf_op jit(solution)/shard_map/reduce_sum | solution.py:50
  93.5 1.1 add_convert_fusion
  94.7 19.3 %all-gather.14.cloned.1.call-done = bf16[2,4608,64]{1,2,0:T(8,128)(2,1)} async-done(((bf16[2,2304,64]{1,2,0:T(8,128)(2,1)}), bf16[2,4608,64]{1,2,0:T(8,128)(2,1)}) %all-gather.14.cloned.1.call-update) | async-done | bytes 1179664 | tf_op jit(solution)/shard_map/all_gather | solution.py:106
  114.0 1.8 fusion.42
  115.8 1.6 collective-permute-start
  117.3 0.6 fusion.14
  117.9 0.6 collective-permute-start.1
  118.5 19.6 %all-gather.10.cloned.1.call-done = bf16[4608,128]{0,1:T(8,128)(2,1)} async-done(((bf16[2304,128]{0,1:T(8,128)(2,1)}), bf16[4608,128]{0,1:T(8,128)(2,1)}) %all-gather.10.cloned.1.call-update) | async-done | bytes 1179664 | tf_op jit(solution)/shard_map/all_gather | solution.py:105
  138.2 1.8 fusion.40
  140.0 0.2 fusion.28
  140.3 16.4 %all_gather.31 = bf16[1024,128]{0,1:T(8,128)(2,1)S(1)} all-gather(bf16[128,128]{0,1:T(8,128)(2,1)S(1)} %pad_maximum_fusion), channel_id=1, replica_groups=mesh['task'=4,'tensor'=4,'dp'=2] {'task','dp'}, dimensions={0}, use_global_device_ids=true | all-gather | bytes 294912 | tf_op jit(solution)/shard_map/all_gather | solution.py:143
  156.7 17.9 %all_gather.32 = bf16[1024,128]{0,1:T(8,128)(2,1)S(1)} all-gather(bf16[128,128]{0,1:T(8,128)(2,1)S(1)} %fusion.19), channel_id=1, replica_groups=mesh['task'=4,'tensor'=4,'dp'=2] {'task','dp'}, dimensions={0}, use_global_device_ids=true | all-gather | bytes 294912 | tf_op jit(solution)/shard_map/all_gather | solution.py:144
  174.6 0.4 fusion.43
  175.1 3.1 convolution_convert_fusion
  178.2 0.2 convert_element_type.132
  178.5 29.1 %reduce-scatter.2.cloned.1.call-done = bf16[32,4608]{1,0:T(8,128)(2,1)} async-done(((bf16[128,4608]{1,0:T(8,128)(2,1)}), bf16[32,4608]{1,0:T(8,128)(2,1)}) %reduce-scatter.2.cloned.1.call-update) | async-done | bytes 294928 | tf_op jit(solution)/shard_map/reduce_scatter | solution.py:163
  207.6 1.2 fusion.11
  208.9 1.3 multiply_reduce_fusion.1
  210.2 0.9 multiply_convert_fusion.1
  211.2 0.1 eq.126
  211.4 0.1 convert_element_type.168
  211.5 0.6 convert_reduce_fusion.6
  212.1 79.2 %all-gather.20.cloned.1.call-done = bf16[1024,4608]{1,0:T(8,128)(2,1)} async-done(((bf16[32,4608]{1,0:T(8,128)(2,1)}), bf16[1024,4608]{1,0:T(8,128)(2,1)}) %all-gather.20.cloned.1.call-update) | async-done | bytes 9437200 | tf_op jit(solution)/shard_map/all_gather | solution.py:171
  291.3 14.4 %exponential_reduce_fusion = (f32[1024]{0:T(1024)S(1)}, f32[1024]{0:T(1024)S(1)}) fusion(s32[896]{0:T(1024)S(1)} %iota_add_fusion, s32[1024]{0:T(1024)S(1)} %eq.126, bf16[1024,4608]{1,0:T(8,128)(2,1)} %all-gather.20.cloned.1.call-done, bf16[896,4608]{1,0:T(8,128)(2,1)} %param.35), kind=kOutput, calls=%fused_computation.8 | convolution fusion | flops 8461219840 | bytes 17710592 | tf_op jit(solution)/shard_map/dot_general | solution.py:178
  305.7 20.1 %all-reduce = (f32[1024]{0:T(1024)S(1)}, f32[1024]{0:T(1024)S(1)}) all-reduce(f32[1024]{0:T(1024)S(1)} %get-tuple-element.3, f32[1024]{0:T(1024)S(1)} %get-tuple-element.2), channel_id=1, replica_groups=mesh['task'=4,'tensor'=4,'dp'=2] {'tensor','dp'}, use_global_device_ids=true, to_apply=%region_15.16 | all-reduce | flops 2048 | bytes 16384 | tf_op jit(solution)/shard_map/psum | solution.py:18
  325.8 6.1 %all-reduce.1 = (f32[1024]{0:T(1024)S(1)}, f32[1024]{0:T(1024)S(1)}) all-reduce(f32[1024]{0:T(1024)S(1)} %get-tuple-element.10, f32[1024]{0:T(1024)S(1)} %get-tuple-element.11), channel_id=1, replica_groups=mesh['task'=4,'tensor'=4,'dp'=2] {'task'}, use_global_device_ids=true, to_apply=%region_16.17 | all-reduce | flops 2048 | bytes 16384 | tf_op jit(solution)/shard_map/psum | solution.py:18
  332.0 0.7 fusion.41
  332.8 0.6 dynamic_slice.7
  333.4 1.8 pad_maximum_fusion.1
  (76 shorter events, 1.3 us)
Async XLA Ops:
  7.2 4.5 %copy-start.11 = (s32[36,2]{0,1:T(2,128)S(1)}, s32[36,2]{0,1:T(2,128)}, u32[]{:S(2)}) copy-start(s32[36,2]{0,1:T(2,128)} %param.30) | copy-start | bytes 868
  7.2 31.3 %all-gather.12.cloned.1.call-start = ((), (), s32[]{:S(2)}) async-start(), calls=%async_computation.3 | async-start | bytes 2949120 | tf_op jit(solution)/shard_map/all_gather | solution.py:96
  11.6 52.6 %all-gather.8.cloned.1.call-start = ((), (), s32[]{:S(2)}) async-start(), calls=%async_computation.1 | async-start | bytes 2949120 | tf_op jit(solution)/shard_map/all_gather | solution.py:95
  13.7 0.7 copy-start.15
  14.4 1.1 copy-start.4
  16.3 1.2 copy-start.12
  17.5 72.3 %all-gather.16.cloned.1.call-start = ((), (), s32[]{:S(2)}) async-start(), calls=%async_computation.5 | async-start | bytes 2949120 | tf_op jit(solution)/shard_map/all_gather | solution.py:97
  19.6 0.7 copy-start.16
  20.3 1.1 copy-start.6
  21.4 1.5 copy-start.5
  22.7 1.3 copy-start
  22.8 91.2 %all-gather.14.cloned.1.call-start = ((), (), s32[]{:S(2)}) async-start(), calls=%async_computation.4 | async-start | bytes 1769472 | tf_op jit(solution)/shard_map/all_gather | solution.py:106
  24.3 17.8 %copy-start.2 = (bf16[2,2304,64]{1,2,0:T(8,128)(2,1)S(1)}, bf16[2,2304,64]{1,2,0:T(8,128)(2,1)}, u32[]{:S(2)}) copy-start(bf16[2,2304,64]{1,2,0:T(8,128)(2,1)} %param.22) | copy-start | bytes 1769476
  43.3 94.9 %all-gather.10.cloned.1.call-start = ((), (), s32[]{:S(2)}) async-start(), calls=%async_computation.2 | async-start | bytes 1769472 | tf_op jit(solution)/shard_map/all_gather | solution.py:105
  73.0 102.1 %all-gather.18.cloned.1.call-start = ((), (), s32[]{:S(2)}) async-start(), calls=%async_computation.6 | async-start | bytes 1769472 | tf_op jit(solution)/shard_map/all_gather | solution.py:107
  73.1 20.4 %copy-start.3 = (bf16[128,2304]{1,0:T(8,128)(2,1)S(1)}, bf16[128,2304]{1,0:T(8,128)(2,1)}, u32[]{:S(2)}) copy-start(bf16[128,2304]{1,0:T(8,128)(2,1)} %param.23) | copy-start | bytes 1769476
  93.4 20.5 %copy-start.14 = (f32[4608]{0:T(1024)S(1)}, f32[4608]{0:T(1024)}, u32[]{:S(2)}) copy-start(f32[4608]{0:T(1024)} %param.20) | copy-start | bytes 55300
  94.6 113.0 %reduce-scatter.2.cloned.1.call-start = ((), (), s32[]{:S(2)}) async-start(), calls=%async_computation.7 | async-start | bytes 1474560 | tf_op jit(solution)/shard_map/reduce_scatter | solution.py:163
  114.0 3.3 copy-start.13
  115.8 24.2 %collective-permute-start = (bf16[128,64]{0,1:T(8,128)(2,1)S(1)}, bf16[128,64]{0,1:T(8,128)(2,1)S(1)}, u32[]{:S(2)}, u32[]{:S(2)}) collective-permute-start(bf16[128,64]{0,1:T(8,128)(2,1)S(1)} %get-tuple-element.22), channel_id=1, source_target_pairs={{0,2},{2,0},{4,6},{6,4},{1,3},{3,1},{5,7},{7,5},{8,10},{10,8},{12,... | collective-permute-start | bytes 49160 | tf_op jit(solution)/shard_map/ppermute | solution.py:29
  117.9 38.8 %collective-permute-start.1 = (bf16[128,64]{0,1:T(8,128)(2,1)S(1)}, bf16[128,64]{0,1:T(8,128)(2,1)S(1)}, u32[]{:S(2)}, u32[]{:S(2)}) collective-permute-start(bf16[128,64]{0,1:T(8,128)(2,1)S(1)} %fusion.14), channel_id=1, source_target_pairs={{0,2},{2,0},{4,6},{6,4},{1,3},{3,1},{5,7},{7,5},{8,10},{10,8},{12,... | collective-permute-start | bytes 49160 | tf_op jit(solution)/shard_map/ppermute | solution.py:29
  178.2 113.2 %all-gather.20.cloned.1.call-start = ((), (), s32[]{:S(2)}) async-start(), calls=%async_computation.8 | async-start | bytes 9732096 | tf_op jit(solution)/shard_map/all_gather | solution.py:171
  178.5 31.7 %copy-start.7 = (f32[4608]{0:T(1024)S(1)}, f32[4608]{0:T(1024)}, u32[]{:S(2)}) copy-start(f32[4608]{0:T(1024)} %param.33) | copy-start | bytes 55300
  178.5 31.7 %copy-start.8 = (f32[4608]{0:T(1024)S(1)}, f32[4608]{0:T(1024)}, u32[]{:S(2)}) copy-start(f32[4608]{0:T(1024)} %param.34) | copy-start | bytes 55300
  207.6 2.5 copy-start.1
  208.8 2.3 copy-start.10
  208.8 2.5 copy-start.9
Sparse Core Ops, SparseCore 0:
  11.7 26.7 all-gather.11
  40.1 24.0 all-gather.7
  65.7 24.0 all-gather.15
  91.2 22.7 all-gather.13
  115.4 22.7 all-gather.9
  139.6 24.4 all-gather.17
  178.3 29.2 reduce-scatter.1
  211.2 80.0 all-gather.19
